TPU v7x, 32 devices: a whole 2x2x4 slice. The times are simulated.
32 devices in a mesh: segment: 2 (over core), gx: 2 (over x), gy: 4 (over z), gz: 2 (over y).
Axes of the slice: x: 2, y: 2, z: 4, core: 2. Of those that a mesh axis runs over, the one named last changes fastest.
Arguments:
- features: bfloat16 [2, 16, 8, 128, 256], P(None, None, 'gx', 'gy', 'gz'), may hold values from -6 to 6
- weights: bfloat16 [2, 2, 16, 16, 3, 3, 3], P('segment'), may hold values from -0.4375 to 0.4375
- biases: bfloat16 [2, 2, 16], P('segment'), may hold values from -3 to 3
Outputs:
- section_out: bfloat16 [2, 2, 16, 8, 128, 256], P('segment', None, None, 'gx', 'gy', 'gz')
All inputs are finite; a program needn't handle non-finite values.
Results may differ from a plain program's by a relative error of at most 0.0054.
Values may be sent and summed in bfloat16 or wider, within the bound.
No kernel may reach another device: no remote copies, remote signals or barrier semaphores. Data moves between devices by JAX's collectives and lax.ppermute only.
A program may use at most 64 MiB of HBM per device.

v0:
```python
import jax
import jax.numpy as jnp
from jax import lax
from jax.sharding import PartitionSpec as P


def with_halo(value, sides, width):
    for axis, dim in sides:
        size, length = (lax.axis_size(axis), value.shape[dim])
        up = [(i, (i + 1) % size) for i in range(size - 1)]
        down = [(j, i) for i, j in up]
        last = lax.slice_in_dim(value, length - width, length, axis=dim)
        initial = lax.slice_in_dim(value, 0, width, axis=dim)
        before = lax.ppermute(last, axis, up)
        after = lax.ppermute(initial, axis, down)
        value = jnp.concatenate([before, value, after], axis=dim)
    return value


def band_table(width):
    source = lax.broadcasted_iota(jnp.int32, (width + 2, 3, width), 0)
    offsets = lax.broadcasted_iota(jnp.int32, (width + 2, 3, width), 1)
    target = lax.broadcasted_iota(jnp.int32, (width + 2, 3, width), 2)
    return jnp.where(source == target + offsets, 1.0, 0.0).astype(jnp.bfloat16)


def convolve(field, kernel, offset):
    padded = with_halo(field, (("gx", 1), ("gy", 2), ("gz", 3)), 1)
    depth = field.shape[1]
    height = field.shape[2]
    width = field.shape[3]
    shifted = jnp.einsum(
        "cxyw,wdz->dcxyz", padded, band_table(width), preferred_element_type=jnp.float32
    ).astype(jnp.bfloat16)
    linear = jnp.zeros((kernel.shape[0], depth, height, width), jnp.float32)
    for step_x in range(3):
        for step_y in range(3):
            slab = shifted[:, :, step_x : step_x + depth, step_y : step_y + height, :]
            taps = kernel[:, :, step_x, step_y, :]
            linear = linear + jnp.einsum(
                "oid,dixyz->oxyz", taps, slab, preferred_element_type=jnp.float32
            )
    summed = linear + offset.astype(jnp.float32)[:, None, None, None]
    return jnp.where(summed > 0, summed, 0.2 * summed).astype(jnp.bfloat16)


def section_pass(field, kernels, offsets):
    return convolve(convolve(field, kernels[0], offsets[0]), kernels[1], offsets[1])


def shards(features, weights, biases):
    section = lax.axis_index("segment")
    micro_count = features.shape[0]
    all_kernels, all_offsets = (
        lax.all_gather(weights, "segment", axis=0, tiled=True),
        lax.all_gather(biases, "segment", axis=0, tiled=True),
    )
    half_count = micro_count // 2
    my_batches = lax.dynamic_slice_in_dim(features, section * half_count, half_count, 0)
    hidden = section_pass(my_batches[0], all_kernels[0], all_offsets[0])
    first_list = [hidden]
    hidden = section_pass(hidden, all_kernels[1], all_offsets[1])
    second_list = [hidden]
    stacked = jnp.stack([jnp.stack(first_list), jnp.stack(second_list)])
    return lax.all_to_all(stacked, "segment", split_axis=0, concat_axis=1, tiled=True)


def solution(mesh):
    placed = (
        P(None, None, "gx", "gy", "gz"),
        P("segment", None, None, None, None, None, None),
        P("segment", None, None),
    )
    return jax.shard_map(
        shards,
        mesh=mesh,
        in_specs=placed,
        out_specs=P("segment", None, None, "gx", "gy", "gz"),
        check_vma=False,
    )
```

profile of v0, /device:TPU:0, one launch (start us, length us, event | category | flops | bytes accessed | tf_op | source)
XLA Modules:
  0.0 191.6 jit_solution(2719549731387878683)
XLA Ops:
  0.0 1.2 copy-done
  1.3 4.9 %collective-permute-start = (bf16[16,1,32,128]{3,2,1,0:T(8,128)(2,1)S(1)}, bf16[16,1,32,128]{3,2,1,0:T(8,128)(2,1)S(1)}, u32[]{:S(2)}, u32[]{:S(2)}) collective-permute-start(bf16[16,1,32,128]{3,2,1,0:T(8,128)(2,1)S(1)} %get-tuple-element.63), channel_id=1, source_target_pairs={{0,8},{1,9},{2,10},{3,11},{4,12},{5,13},{6,14},{7,15},{16,24},{17,... | collective-permute-start | bytes 393224 | tf_op jit(solution)/shard_map/ppermute | solution.py:14
  6.2 1.3 collective-permute-start.1
  7.5 2.1 %all_gather.6 = bf16[2,2,16,16,3,3,3]{3,2,6,5,4,1,0:T(8,128)(2,1)S(1)} all-gather(bf16[1,2,16,16,3,3,3]{3,2,6,5,4,1,0:T(8,128)(2,1)S(1)} %copy-done.2), channel_id=1, replica_groups=mesh['segment'=2,'gx'=2,'gy'=4,'gz'=2] {'segment'}, dimensions={0}, use_global_device_ids=true | all-gather | bytes 82944 | tf_op jit(solution)/shard_map/all_gather | solution.py:55
  9.6 3.4 %collective-permute-done.1 = bf16[16,1,32,128]{3,2,1,0:T(8,128)(2,1)S(1)} collective-permute-done((bf16[16,1,32,128]{3,2,1,0:T(8,128)(2,1)S(1)}, bf16[16,1,32,128]{3,2,1,0:T(8,128)(2,1)S(1)}, u32[]{:S(2)}, u32[]{:S(2)}) %collective-permute-start.1) | collective-permute-done | bytes 131104 | tf_op jit(solution)/shard_map/ppermute | solution.py:15
  13.1 3.5 %collective-permute-start.2 = (bf16[16,6,1,128]{3,2,1,0:T(2,128)(2,1)S(1)}, bf16[16,6,1,128]{3,2,1,0:T(2,128)(2,1)S(1)}, u32[]{:S(2)}, u32[]{:S(2)}) collective-permute-start(bf16[16,6,1,128]{3,2,1,0:T(2,128)(2,1)S(1)} %get-tuple-element.55), channel_id=1, source_target_pairs={{0,2},{2,4},{4,6},{1,3},{3,5},{5,7},{8,10},{10,12},{12,14},{9,11},... | collective-permute-start | bytes 73736 | tf_op jit(solution)/shard_map/ppermute | solution.py:14
  16.6 1.3 collective-permute-start.3
  18.0 1.8 all_gather.7
  19.8 2.8 %collective-permute-done.3 = bf16[16,6,1,128]{3,2,1,0:T(2,128)(2,1)S(1)} collective-permute-done((bf16[16,6,1,128]{3,2,1,0:T(2,128)(2,1)S(1)}, bf16[16,6,1,128]{3,2,1,0:T(2,128)(2,1)S(1)}, u32[]{:S(2)}, u32[]{:S(2)}) %collective-permute-start.3) | collective-permute-done | bytes 24608 | tf_op jit(solution)/shard_map/ppermute | solution.py:15
  24.9 1.3 collective-permute-start.5
  26.2 4.5 %collective-permute-start.4 = (bf16[16,6,34,1]{2,0,3,1:T(8,128)(2,1)S(1)}, bf16[16,6,34,1]{2,0,3,1:T(8,128)(2,1)S(1)}, u32[]{:S(2)}, u32[]{:S(2)}) collective-permute-start(bf16[16,6,34,1]{2,0,3,1:T(8,128)(2,1)S(1)} %copy.44), channel_id=1, source_target_pairs={{0,1},{2,3},{4,5},{6,7},{8,9},{10,11},{12,13},{14,15},{16,17},{18,... | collective-permute-start | bytes 19592 | tf_op jit(solution)/shard_map/ppermute | solution.py:14
  30.8 1.5 collective-permute-done.4
  33.8 2.9 %convert_bitcast_fusion.3 = bf16[3,16,6,34,128]{4,3,2,1,0:T(8,128)(2,1)S(1)} fusion(bf16[16,6,34,1]{3,2,1,0:T(8,128)(2,1)S(1)} %copy.47, bf16[16,6,1,128]{3,2,1,0:T(2,128)(2,1)S(1)} %collective-permute-done.3, bf16[16,1,32,128]{3,2,1,0:T(8,128)(2,1)S(1)} %collective-permute-done.1, bf16[16,4,32,128]{3,2,1,0:T(8,128)(2,1)S(1)} %dynamic-slice_bitcast_fusion, ...), kind=kOutput, calls=%fused_computation.7 | convolution fusion | flops 333271296 | bytes 3355392 | tf_op jit(solution)/shard_map/cxyw,wdz->dcxyz/dot_general | solution.py:32
  36.7 3.7 %fusion.370 = (bf16[3,16,4,32,128]{4,3,2,1,0:T(8,128)(2,1)S(1)}, bf16[3,16,4,32,128]{4,3,2,1,0:T(8,128)(2,1)S(1)}, bf16[3,16,4,32,128]{4,3,2,1,0:T(8,128)(2,1)S(...) fusion(bf16[3,16,6,34,128]{4,3,2,1,0:T(8,128)(2,1)S(1)} %conver, ...), kind=kLoop, calls=%fused_computation.272 | loop fusion | bytes 28311552 | tf_op jit(solution)/shard_map/slice | solution.py:38
  41.4 1.1 fusion.323
  42.5 1.1 fusion.320
  43.6 1.1 fusion.317
  45.7 1.1 fusion.311
  47.9 1.1 fusion.305
  48.9 1.1 fusion.326
  50.1 1.5 collective-permute-start.6
  51.6 1.3 collective-permute-start.7
  52.9 1.2 collective-permute-done.6
  54.1 4.4 %collective-permute-done.7 = bf16[16,1,32,128]{3,0,2,1:T(8,128)(2,1)S(1)} collective-permute-done((bf16[16,1,32,128]{3,0,2,1:T(8,128)(2,1)S(1)}, bf16[16,1,32,128]{3,0,2,1:T(8,128)(2,1)S(1)}, u32[]{:S(2)}, u32[]{:S(2)}) %collective-permute-start.7) | collective-permute-done | bytes 131104 | tf_op jit(solution)/shard_map/ppermute | solution.py:15
  58.4 3.5 %collective-permute-start.8 = (bf16[16,6,1,128]{3,0,2,1:T(8,128)(2,1)S(1)}, bf16[16,6,1,128]{3,0,2,1:T(8,128)(2,1)S(1)}, u32[]{:S(2)}, u32[]{:S(2)}) collective-permute-start(bf16[16,6,1,128]{3,0,2,1:T(8,128)(2,1)S(1)} %get-tuple-element.53), channel_id=1, source_target_pairs={{0,2},{2,4},{4,6},{1,3},{3,5},{5,7},{8,10},{10,12},{12,14},{9,11},... | collective-permute-start | bytes 73736 | tf_op jit(solution)/shard_map/ppermute | solution.py:14
  61.9 1.5 collective-permute-start.9
  63.5 4.2 %collective-permute-done.9 = bf16[16,6,1,128]{3,0,2,1:T(8,128)(2,1)S(1)} collective-permute-done((bf16[16,6,1,128]{3,0,2,1:T(8,128)(2,1)S(1)}, bf16[16,6,1,128]{3,0,2,1:T(8,128)(2,1)S(1)}, u32[]{:S(2)}, u32[]{:S(2)}) %collective-permute-start.9) | collective-permute-done | bytes 24608 | tf_op jit(solution)/shard_map/ppermute | solution.py:15
  69.1 4.2 %collective-permute-start.10 = (bf16[16,6,34,1]{2,0,3,1:T(8,128)(2,1)S(1)}, bf16[16,6,34,1]{2,0,3,1:T(8,128)(2,1)S(1)}, u32[]{:S(2)}, u32[]{:S(2)}) collective-permute-start(bf16[16,6,34,1]{2,0,3,1:T(8,128)(2,1)S(1)} %copy.57), channel_id=1, source_target_pairs={{0,1},{2,3},{4,5},{6,7},{8,9},{10,11},{12,13},{14,15},{16,17},{18,... | collective-permute-start | bytes 19592 | tf_op jit(solution)/shard_map/ppermute | solution.py:14
  74.2 1.3 collective-permute-start.11
  76.3 3.6 %collective-permute-done.11 = bf16[16,6,34,1]{2,0,3,1:T(8,128)(2,1)S(1)} collective-permute-done((bf16[16,6,34,1]{2,0,3,1:T(8,128)(2,1)S(1)}, bf16[16,6,34,1]{2,0,3,1:T(8,128)(2,1)S(1)}, u32[]{:S(2)}, u32[]{:S(2)}) %collective-permute-start.11) | collective-permute-done | bytes 6560 | tf_op jit(solution)/shard_map/ppermute | solution.py:15
  80.7 1.9 pad_maximum_fusion
  82.6 1.4 convert_bitcast_fusion.2
  84.0 4.1 %fusion.369 = (bf16[3,16,4,32,128]{4,3,2,1,0:T(8,128)(2,1)S(1)}, bf16[3,16,4,32,128]{4,3,2,1,0:T(8,128)(2,1)S(1)}, bf16[3,16,4,32,128]{4,3,2,1,0:T(8,128)(2,1)S(...) fusion(bf16[3,16,6,34,128]{4,3,2,1,0:T(8,128)(2,1)S(1)} %conver, ...), kind=kLoop, calls=%fused_computation.271 | loop fusion | bytes 28311552 | tf_op jit(solution)/shard_map/slice | solution.py:38
  96.6 1.1 fusion.329
  97.7 1.5 collective-permute-start.12
  99.2 1.3 collective-permute-start.13
  100.5 1.2 collective-permute-done.12
  101.7 4.4 %collective-permute-done.13 = bf16[16,1,32,128]{3,0,2,1:T(8,128)(2,1)S(1)} collective-permute-done((bf16[16,1,32,128]{3,0,2,1:T(8,128)(2,1)S(1)}, bf16[16,1,32,128]{3,0,2,1:T(8,128)(2,1)S(1)}, u32[]{:S(2)}, u32[]{:S(2)}) %collective-permute-start.13) | collective-permute-done | bytes 131104 | tf_op jit(solution)/shard_map/ppermute | solution.py:15
  106.1 3.5 %collective-permute-start.14 = (bf16[16,6,1,128]{3,0,2,1:T(8,128)(2,1)S(1)}, bf16[16,6,1,128]{3,0,2,1:T(8,128)(2,1)S(1)}, u32[]{:S(2)}, u32[]{:S(2)}) collective-permute-start(bf16[16,6,1,128]{3,0,2,1:T(8,128)(2,1)S(1)} %get-tuple-element.51), channel_id=1, source_target_pairs={{0,2},{2,4},{4,6},{1,3},{3,5},{5,7},{8,10},{10,12},{12,14},{9,11},... | collective-permute-start | bytes 73736 | tf_op jit(solution)/shard_map/ppermute | solution.py:14
  109.6 1.3 collective-permute-start.15
  111.1 4.2 %collective-permute-done.15 = bf16[16,6,1,128]{3,0,2,1:T(8,128)(2,1)S(1)} collective-permute-done((bf16[16,6,1,128]{3,0,2,1:T(8,128)(2,1)S(1)}, bf16[16,6,1,128]{3,0,2,1:T(8,128)(2,1)S(1)}, u32[]{:S(2)}, u32[]{:S(2)}) %collective-permute-start.15) | collective-permute-done | bytes 24608 | tf_op jit(solution)/shard_map/ppermute | solution.py:15
  116.7 1.6 collective-permute-start.16
  119.2 1.5 collective-permute-start.17
  121.5 3.4 %collective-permute-done.17 = bf16[16,6,34,1]{2,0,3,1:T(8,128)(2,1)S(1)} collective-permute-done((bf16[16,6,34,1]{2,0,3,1:T(8,128)(2,1)S(1)}, bf16[16,6,34,1]{2,0,3,1:T(8,128)(2,1)S(1)}, u32[]{:S(2)}, u32[]{:S(2)}) %collective-permute-start.17) | collective-permute-done | bytes 6560 | tf_op jit(solution)/shard_map/ppermute | solution.py:15
  125.8 1.9 pad_maximum_fusion.1
  127.7 1.4 convert_bitcast_fusion.1
  129.0 3.7 %fusion.368 = (bf16[3,16,4,32,128]{4,3,2,1,0:T(8,128)(2,1)S(1)}, bf16[3,16,4,32,128]{4,3,2,1,0:T(8,128)(2,1)S(1)}, bf16[3,16,4,32,128]{4,3,2,1,0:T(8,128)(2,1)S(...) fusion(bf16[3,16,6,34,128]{4,3,2,1,0:T(8,128)(2,1)S(1)} %conver, ...), kind=kLoop, calls=%fused_computation.270 | loop fusion | bytes 28311552 | tf_op jit(solution)/shard_map/slice | solution.py:38
  141.2 1.1 fusion.332
  142.3 1.5 collective-permute-start.18
  143.8 1.3 collective-permute-start.19
  145.1 1.2 collective-permute-done.18
  146.3 4.4 %collective-permute-done.19 = bf16[16,1,32,128]{3,0,2,1:T(8,128)(2,1)S(1)} collective-permute-done((bf16[16,1,32,128]{3,0,2,1:T(8,128)(2,1)S(1)}, bf16[16,1,32,128]{3,0,2,1:T(8,128)(2,1)S(1)}, u32[]{:S(2)}, u32[]{:S(2)}) %collective-permute-start.19) | collective-permute-done | bytes 131104 | tf_op jit(solution)/shard_map/ppermute | solution.py:15
  150.7 1.9 %collective-permute-start.20 = (bf16[16,6,1,128]{3,0,2,1:T(8,128)(2,1)S(1)}, bf16[16,6,1,128]{3,0,2,1:T(8,128)(2,1)S(1)}, u32[]{:S(2)}, u32[]{:S(2)}) collective-permute-start(bf16[16,6,1,128]{3,0,2,1:T(8,128)(2,1)S(1)} %get-tuple-element.49), channel_id=1, source_target_pairs={{0,2},{2,4},{4,6},{1,3},{3,5},{5,7},{8,10},{10,12},{12,14},{9,11},... | collective-permute-start | bytes 73736 | tf_op jit(solution)/shard_map/ppermute | solution.py:14
  152.6 1.3 collective-permute-start.21
  154.1 4.2 %collective-permute-done.21 = bf16[16,6,1,128]{3,0,2,1:T(8,128)(2,1)S(1)} collective-permute-done((bf16[16,6,1,128]{3,0,2,1:T(8,128)(2,1)S(1)}, bf16[16,6,1,128]{3,0,2,1:T(8,128)(2,1)S(1)}, u32[]{:S(2)}, u32[]{:S(2)}) %collective-permute-start.21) | collective-permute-done | bytes 24608 | tf_op jit(solution)/shard_map/ppermute | solution.py:15
  159.8 1.6 collective-permute-start.22
  162.2 1.5 collective-permute-start.23
  164.6 3.4 %collective-permute-done.23 = bf16[16,6,34,1]{2,0,3,1:T(8,128)(2,1)S(1)} collective-permute-done((bf16[16,6,34,1]{2,0,3,1:T(8,128)(2,1)S(1)}, bf16[16,6,34,1]{2,0,3,1:T(8,128)(2,1)S(1)}, u32[]{:S(2)}, u32[]{:S(2)}) %collective-permute-start.23) | collective-permute-done | bytes 6560 | tf_op jit(solution)/shard_map/ppermute | solution.py:15
  168.8 1.9 pad_maximum_fusion.2
  170.7 1.4 convert_bitcast_fusion
  172.1 3.7 %fusion.367 = (bf16[3,16,4,32,128]{4,3,2,1,0:T(8,128)(2,1)S(1)}, bf16[3,16,4,32,128]{4,3,2,1,0:T(8,128)(2,1)S(1)}, bf16[3,16,4,32,128]{4,3,2,1,0:T(8,128)(2,1)S(...) fusion(bf16[3,16,6,34,128]{4,3,2,1,0:T(8,128)(2,1)S(1)} %conver, ...), kind=kLoop, calls=%fused_computation.269 | loop fusion | bytes 28311552 | tf_op jit(solution)/shard_map/slice | solution.py:38
  184.2 1.1 fusion.338
  185.4 4.7 %all_to_all.12 = bf16[2,1,16,4,32,128]{5,2,4,3,1,0:T(8,128)(2,1)S(1)} all-to-all(bf16[2,1,16,4,32,128]{5,2,4,3,1,0:T(8,128)(2,1)S(1)} %pad_maximum_fusion.3), channel_id=1, replica_groups=mesh['segment'=2,'gx'=2,'gy'=4,'gz'=2] {'segment'}, dimensions={0} | all-to-all | bytes 2097152 | tf_op jit(solution)/shard_map/all_to_all | solution.py:65
  190.1 1.2 copy.99
  (79 shorter events, 45.0 us)
Async XLA Ops:
  0.0 1.2 copy-start
  0.0 7.5 %copy-start.2 = (bf16[1,2,16,16,3,3,3]{3,2,6,5,4,1,0:T(8,128)(2,1)S(1)}, bf16[1,2,16,16,3,3,3]{3,2,6,5,4,1,0:T(8,128)(2,1)}, u32[]{:S(2)}) copy-start(bf16[1,2,16,16,3,3,3]{3,2,6,5,4,1,0:T(8,128)(2,1)} %param.4) | copy-start | bytes 82948
  1.3 16.7 %copy-start.3 = (bf16[1,2,16]{2,1,0:T(2,128)(2,1)S(1)}, bf16[1,2,16]{2,1,0:T(2,128)(2,1)}, u32[]{:S(2)}) copy-start(bf16[1,2,16]{2,1,0:T(2,128)(2,1)} %param.5) | copy-start | bytes 196
  1.3 8.3 %collective-permute-start = (bf16[16,1,32,128]{3,2,1,0:T(8,128)(2,1)S(1)}, bf16[16,1,32,128]{3,2,1,0:T(8,128)(2,1)S(1)}, u32[]{:S(2)}, u32[]{:S(2)}) collective-permute-start(bf16[16,1,32,128]{3,2,1,0:T(8,128)(2,1)S(1)} %get-tuple-element.63), channel_id=1, source_target_pairs={{0,8},{1,9},{2,10},{3,11},{4,12},{5,13},{6,14},{7,15},{16,24},{17,... | collective-permute-start | bytes 393224 | tf_op jit(solution)/shard_map/ppermute | solution.py:14
  6.2 6.9 %collective-permute-start.1 = (bf16[16,1,32,128]{3,2,1,0:T(8,128)(2,1)S(1)}, bf16[16,1,32,128]{3,2,1,0:T(8,128)(2,1)S(1)}, u32[]{:S(2)}, u32[]{:S(2)}) collective-permute-start(bf16[16,1,32,128]{3,2,1,0:T(8,128)(2,1)S(1)} %get-tuple-element.64), channel_id=1, source_target_pairs={{8,0},{9,1},{10,2},{11,3},{12,4},{13,5},{14,6},{15,7},{24,16},{25,... | collective-permute-start | bytes 393224 | tf_op jit(solution)/shard_map/ppermute | solution.py:15
  13.1 6.7 %collective-permute-start.2 = (bf16[16,6,1,128]{3,2,1,0:T(2,128)(2,1)S(1)}, bf16[16,6,1,128]{3,2,1,0:T(2,128)(2,1)S(1)}, u32[]{:S(2)}, u32[]{:S(2)}) collective-permute-start(bf16[16,6,1,128]{3,2,1,0:T(2,128)(2,1)S(1)} %get-tuple-element.55), channel_id=1, source_target_pairs={{0,2},{2,4},{4,6},{1,3},{3,5},{5,7},{8,10},{10,12},{12,14},{9,11},... | collective-permute-start | bytes 73736 | tf_op jit(solution)/shard_map/ppermute | solution.py:14
  16.6 6.0 %collective-permute-start.3 = (bf16[16,6,1,128]{3,2,1,0:T(2,128)(2,1)S(1)}, bf16[16,6,1,128]{3,2,1,0:T(2,128)(2,1)S(1)}, u32[]{:S(2)}, u32[]{:S(2)}) collective-permute-start(bf16[16,6,1,128]{3,2,1,0:T(2,128)(2,1)S(1)} %get-tuple-element.56), channel_id=1, source_target_pairs={{2,0},{4,2},{6,4},{3,1},{5,3},{7,5},{10,8},{12,10},{14,12},{11,9},... | collective-permute-start | bytes 73736 | tf_op jit(solution)/shard_map/ppermute | solution.py:15
  24.9 8.1 %collective-permute-start.5 = (bf16[16,6,34,1]{2,0,3,1:T(8,128)(2,1)S(1)}, bf16[16,6,34,1]{2,0,3,1:T(8,128)(2,1)S(1)}, u32[]{:S(2)}, u32[]{:S(2)}) collective-permute-start(bf16[16,6,34,1]{2,0,3,1:T(8,128)(2,1)S(1)} %copy.45), channel_id=1, source_target_pairs={{1,0},{3,2},{5,4},{7,6},{9,8},{11,10},{13,12},{15,14},{17,16},{19,... | collective-permute-start | bytes 19592 | tf_op jit(solution)/shard_map/ppermute | solution.py:15
  26.2 6.1 %collective-permute-start.4 = (bf16[16,6,34,1]{2,0,3,1:T(8,128)(2,1)S(1)}, bf16[16,6,34,1]{2,0,3,1:T(8,128)(2,1)S(1)}, u32[]{:S(2)}, u32[]{:S(2)}) collective-permute-start(bf16[16,6,34,1]{2,0,3,1:T(8,128)(2,1)S(1)} %copy.44), channel_id=1, source_target_pairs={{0,1},{2,3},{4,5},{6,7},{8,9},{10,11},{12,13},{14,15},{16,17},{18,... | collective-permute-start | bytes 19592 | tf_op jit(solution)/shard_map/ppermute | solution.py:14
  50.1 4.0 %collective-permute-start.6 = (bf16[16,1,32,128]{3,0,2,1:T(8,128)(2,1)S(1)}, bf16[16,1,32,128]{3,0,2,1:T(8,128)(2,1)S(1)}, u32[]{:S(2)}, u32[]{:S(2)}) collective-permute-start(bf16[16,1,32,128]{3,0,2,1:T(8,128)(2,1)S(1)} %get-tuple-element.61), channel_id=1, source_target_pairs={{0,8},{1,9},{2,10},{3,11},{4,12},{5,13},{6,14},{7,15},{16,24},{17,... | collective-permute-start | bytes 393224 | tf_op jit(solution)/shard_map/ppermute | solution.py:14
  51.6 6.9 %collective-permute-start.7 = (bf16[16,1,32,128]{3,0,2,1:T(8,128)(2,1)S(1)}, bf16[16,1,32,128]{3,0,2,1:T(8,128)(2,1)S(1)}, u32[]{:S(2)}, u32[]{:S(2)}) collective-permute-start(bf16[16,1,32,128]{3,0,2,1:T(8,128)(2,1)S(1)} %get-tuple-element.62), channel_id=1, source_target_pairs={{8,0},{9,1},{10,2},{11,3},{12,4},{13,5},{14,6},{15,7},{24,16},{25,... | collective-permute-start | bytes 393224 | tf_op jit(solution)/shard_map/ppermute | solution.py:15
  58.4 5.0 %collective-permute-start.8 = (bf16[16,6,1,128]{3,0,2,1:T(8,128)(2,1)S(1)}, bf16[16,6,1,128]{3,0,2,1:T(8,128)(2,1)S(1)}, u32[]{:S(2)}, u32[]{:S(2)}) collective-permute-start(bf16[16,6,1,128]{3,0,2,1:T(8,128)(2,1)S(1)} %get-tuple-element.53), channel_id=1, source_target_pairs={{0,2},{2,4},{4,6},{1,3},{3,5},{5,7},{8,10},{10,12},{12,14},{9,11},... | collective-permute-start | bytes 73736 | tf_op jit(solution)/shard_map/ppermute | solution.py:14
  61.9 5.7 %collective-permute-start.9 = (bf16[16,6,1,128]{3,0,2,1:T(8,128)(2,1)S(1)}, bf16[16,6,1,128]{3,0,2,1:T(8,128)(2,1)S(1)}, u32[]{:S(2)}, u32[]{:S(2)}) collective-permute-start(bf16[16,6,1,128]{3,0,2,1:T(8,128)(2,1)S(1)} %get-tuple-element.54), channel_id=1, source_target_pairs={{2,0},{4,2},{6,4},{3,1},{5,3},{7,5},{10,8},{12,10},{14,12},{11,9},... | collective-permute-start | bytes 73736 | tf_op jit(solution)/shard_map/ppermute | solution.py:15
  69.1 6.4 %collective-permute-start.10 = (bf16[16,6,34,1]{2,0,3,1:T(8,128)(2,1)S(1)}, bf16[16,6,34,1]{2,0,3,1:T(8,128)(2,1)S(1)}, u32[]{:S(2)}, u32[]{:S(2)}) collective-permute-start(bf16[16,6,34,1]{2,0,3,1:T(8,128)(2,1)S(1)} %copy.57), channel_id=1, source_target_pairs={{0,1},{2,3},{4,5},{6,7},{8,9},{10,11},{12,13},{14,15},{16,17},{18,... | collective-permute-start | bytes 19592 | tf_op jit(solution)/shard_map/ppermute | solution.py:14
  74.2 5.7 %collective-permute-start.11 = (bf16[16,6,34,1]{2,0,3,1:T(8,128)(2,1)S(1)}, bf16[16,6,34,1]{2,0,3,1:T(8,128)(2,1)S(1)}, u32[]{:S(2)}, u32[]{:S(2)}) collective-permute-start(bf16[16,6,34,1]{2,0,3,1:T(8,128)(2,1)S(1)} %copy.58), channel_id=1, source_target_pairs={{1,0},{3,2},{5,4},{7,6},{9,8},{11,10},{13,12},{15,14},{17,16},{19,... | collective-permute-start | bytes 19592 | tf_op jit(solution)/shard_map/ppermute | solution.py:15
  97.7 4.0 %collective-permute-start.12 = (bf16[16,1,32,128]{3,0,2,1:T(8,128)(2,1)S(1)}, bf16[16,1,32,128]{3,0,2,1:T(8,128)(2,1)S(1)}, u32[]{:S(2)}, u32[]{:S(2)}) collective-permute-start(bf16[16,1,32,128]{3,0,2,1:T(8,128)(2,1)S(1)} %get-tuple-element.59), channel_id=1, source_target_pairs={{0,8},{1,9},{2,10},{3,11},{4,12},{5,13},{6,14},{7,15},{16,24},{17,... | collective-permute-start | bytes 393224 | tf_op jit(solution)/shard_map/ppermute | solution.py:14
  99.2 6.9 %collective-permute-start.13 = (bf16[16,1,32,128]{3,0,2,1:T(8,128)(2,1)S(1)}, bf16[16,1,32,128]{3,0,2,1:T(8,128)(2,1)S(1)}, u32[]{:S(2)}, u32[]{:S(2)}) collective-permute-start(bf16[16,1,32,128]{3,0,2,1:T(8,128)(2,1)S(1)} %get-tuple-element.60), channel_id=1, source_target_pairs={{8,0},{9,1},{10,2},{11,3},{12,4},{13,5},{14,6},{15,7},{24,16},{25,... | collective-permute-start | bytes 393224 | tf_op jit(solution)/shard_map/ppermute | solution.py:15
  106.1 5.0 %collective-permute-start.14 = (bf16[16,6,1,128]{3,0,2,1:T(8,128)(2,1)S(1)}, bf16[16,6,1,128]{3,0,2,1:T(8,128)(2,1)S(1)}, u32[]{:S(2)}, u32[]{:S(2)}) collective-permute-start(bf16[16,6,1,128]{3,0,2,1:T(8,128)(2,1)S(1)} %get-tuple-element.51), channel_id=1, source_target_pairs={{0,2},{2,4},{4,6},{1,3},{3,5},{5,7},{8,10},{10,12},{12,14},{9,11},... | collective-permute-start | bytes 73736 | tf_op jit(solution)/shard_map/ppermute | solution.py:14
  109.6 5.7 %collective-permute-start.15 = (bf16[16,6,1,128]{3,0,2,1:T(8,128)(2,1)S(1)}, bf16[16,6,1,128]{3,0,2,1:T(8,128)(2,1)S(1)}, u32[]{:S(2)}, u32[]{:S(2)}) collective-permute-start(bf16[16,6,1,128]{3,0,2,1:T(8,128)(2,1)S(1)} %get-tuple-element.52), channel_id=1, source_target_pairs={{2,0},{4,2},{6,4},{3,1},{5,3},{7,5},{10,8},{12,10},{14,12},{11,9},... | collective-permute-start | bytes 73736 | tf_op jit(solution)/shard_map/ppermute | solution.py:15
  116.7 4.0 %collective-permute-start.16 = (bf16[16,6,34,1]{2,0,3,1:T(8,128)(2,1)S(1)}, bf16[16,6,34,1]{2,0,3,1:T(8,128)(2,1)S(1)}, u32[]{:S(2)}, u32[]{:S(2)}) collective-permute-start(bf16[16,6,34,1]{2,0,3,1:T(8,128)(2,1)S(1)} %copy.71), channel_id=1, source_target_pairs={{0,1},{2,3},{4,5},{6,7},{8,9},{10,11},{12,13},{14,15},{16,17},{18,... | collective-permute-start | bytes 19592 | tf_op jit(solution)/shard_map/ppermute | solution.py:14
  119.2 5.7 %collective-permute-start.17 = (bf16[16,6,34,1]{2,0,3,1:T(8,128)(2,1)S(1)}, bf16[16,6,34,1]{2,0,3,1:T(8,128)(2,1)S(1)}, u32[]{:S(2)}, u32[]{:S(2)}) collective-permute-start(bf16[16,6,34,1]{2,0,3,1:T(8,128)(2,1)S(1)} %copy.72), channel_id=1, source_target_pairs={{1,0},{3,2},{5,4},{7,6},{9,8},{11,10},{13,12},{15,14},{17,16},{19,... | collective-permute-start | bytes 19592 | tf_op jit(solution)/shard_map/ppermute | solution.py:15
  142.3 4.0 %collective-permute-start.18 = (bf16[16,1,32,128]{3,0,2,1:T(8,128)(2,1)S(1)}, bf16[16,1,32,128]{3,0,2,1:T(8,128)(2,1)S(1)}, u32[]{:S(2)}, u32[]{:S(2)}) collective-permute-start(bf16[16,1,32,128]{3,0,2,1:T(8,128)(2,1)S(1)} %get-tuple-element.57), channel_id=1, source_target_pairs={{0,8},{1,9},{2,10},{3,11},{4,12},{5,13},{6,14},{7,15},{16,24},{17,... | collective-permute-start | bytes 393224 | tf_op jit(solution)/shard_map/ppermute | solution.py:14
  143.8 6.9 %collective-permute-start.19 = (bf16[16,1,32,128]{3,0,2,1:T(8,128)(2,1)S(1)}, bf16[16,1,32,128]{3,0,2,1:T(8,128)(2,1)S(1)}, u32[]{:S(2)}, u32[]{:S(2)}) collective-permute-start(bf16[16,1,32,128]{3,0,2,1:T(8,128)(2,1)S(1)} %get-tuple-element.58), channel_id=1, source_target_pairs={{8,0},{9,1},{10,2},{11,3},{12,4},{13,5},{14,6},{15,7},{24,16},{25,... | collective-permute-start | bytes 393224 | tf_op jit(solution)/shard_map/ppermute | solution.py:15
  150.7 3.4 %collective-permute-start.20 = (bf16[16,6,1,128]{3,0,2,1:T(8,128)(2,1)S(1)}, bf16[16,6,1,128]{3,0,2,1:T(8,128)(2,1)S(1)}, u32[]{:S(2)}, u32[]{:S(2)}) collective-permute-start(bf16[16,6,1,128]{3,0,2,1:T(8,128)(2,1)S(1)} %get-tuple-element.49), channel_id=1, source_target_pairs={{0,2},{2,4},{4,6},{1,3},{3,5},{5,7},{8,10},{10,12},{12,14},{9,11},... | collective-permute-start | bytes 73736 | tf_op jit(solution)/shard_map/ppermute | solution.py:14
  152.6 5.7 %collective-permute-start.21 = (bf16[16,6,1,128]{3,0,2,1:T(8,128)(2,1)S(1)}, bf16[16,6,1,128]{3,0,2,1:T(8,128)(2,1)S(1)}, u32[]{:S(2)}, u32[]{:S(2)}) collective-permute-start(bf16[16,6,1,128]{3,0,2,1:T(8,128)(2,1)S(1)} %get-tuple-element.50), channel_id=1, source_target_pairs={{2,0},{4,2},{6,4},{3,1},{5,3},{7,5},{10,8},{12,10},{14,12},{11,9},... | collective-permute-start | bytes 73736 | tf_op jit(solution)/shard_map/ppermute | solution.py:15
  159.8 4.0 %collective-permute-start.22 = (bf16[16,6,34,1]{2,0,3,1:T(8,128)(2,1)S(1)}, bf16[16,6,34,1]{2,0,3,1:T(8,128)(2,1)S(1)}, u32[]{:S(2)}, u32[]{:S(2)}) collective-permute-start(bf16[16,6,34,1]{2,0,3,1:T(8,128)(2,1)S(1)} %copy.85), channel_id=1, source_target_pairs={{0,1},{2,3},{4,5},{6,7},{8,9},{10,11},{12,13},{14,15},{16,17},{18,... | collective-permute-start | bytes 19592 | tf_op jit(solution)/shard_map/ppermute | solution.py:14
  162.2 5.7 %collective-permute-start.23 = (bf16[16,6,34,1]{2,0,3,1:T(8,128)(2,1)S(1)}, bf16[16,6,34,1]{2,0,3,1:T(8,128)(2,1)S(1)}, u32[]{:S(2)}, u32[]{:S(2)}) collective-permute-start(bf16[16,6,34,1]{2,0,3,1:T(8,128)(2,1)S(1)} %copy.86), channel_id=1, source_target_pairs={{1,0},{3,2},{5,4},{7,6},{9,8},{11,10},{13,12},{15,14},{17,16},{19,... | collective-permute-start | bytes 19592 | tf_op jit(solution)/shard_map/ppermute | solution.py:15
  185.4 6.0 %copy-start.1 = (bf16[2,16,4,32,128]{4,3,2,1,0:T(8,128)(2,1)S(1)}, bf16[2,16,4,32,128]{4,3,2,1,0:T(8,128)(2,1)}, u32[]{:S(2)}) copy-start(bf16[2,16,4,32,128]{4,3,2,1,0:T(8,128)(2,1)} %param.3) | copy-start | bytes 3145732
where the time goes:
time: 195 us; the launch traced here: 192 us
  starting transfers between devices  49.8 us (26%)
  waiting for transfers between devices  47.8 us (25%)
  matrix products  45.5 us (23%)
  local copies, waits for them, and re-layouts  32.2 us (17%)
  blocking collectives  8.64 us (4%)
  other arithmetic  6.92 us (4%)
    ppermute x12, waiting for transfers between devices, with_halo(): after = lax.ppermute(initial, axis, down)  42.3 us
    dot_general x36, matrix products, convolve(): jnp.einsum('oid,dixyz->oxyz', taps, slab, preferred_element_type=jnp.floa...  38.4 us
    ppermute x12, starting transfers between devices, with_halo(): before = lax.ppermute(last, axis, up)  33.7 us
    ppermute x12, starting transfers between devices, with_halo(): after = lax.ppermute(initial, axis, down)  16.1 us
    slice x4, local copies, waits for them, and re-layouts, convolve(): slab = shifted[:, :, step_x:step_x + depth, step_y:step_y + height, :]  15 us
    dot_general x4, matrix products, convolve(): jnp.einsum('cxyw,wdz->dcxyz', padded, band_table(width), preferred_elemen...  7.04 us
    concatenate x7, other arithmetic, with_halo(): value = jnp.concatenate([before, value, after], axis=dim)  6.71 us
    ppermute x12, waiting for transfers between devices, with_halo(): before = lax.ppermute(last, axis, up)  5.5 us
  transfers between devices with their start and end apart: 24, of which 17 were waited for; matrix products, arithmetic and copies ran while one was open for 3% of the time, Pallas kernels for 0%

commit v1 on v0

--- a/solution.py
+++ b/solution.py
@@ -2,6 +2,15 @@
 import jax.numpy as jnp
 from jax import lax
 from jax.sharding import PartitionSpec as P
+
+
+def report_set_here(work_x):
+    side_arr = jax.lax.axis_size("segment")
+    new = jnp.split(work_x, side_arr, 0)
+    f_next = jnp.stack(new)
+    z1 = jax.lax.all_to_all(f_next, "segment", 0, 0)
+    known = jnp.concatenate(z1, 1)
+    return known
 
 
 def with_halo(value, sides, width):
@@ -62,7 +71,7 @@
     hidden = section_pass(hidden, all_kernels[1], all_offsets[1])
     second_list = [hidden]
     stacked = jnp.stack([jnp.stack(first_list), jnp.stack(second_list)])
-    return lax.all_to_all(stacked, "segment", split_axis=0, concat_axis=1, tiled=True)
+    return report_set_here(stacked)
 
 
 def solution(mesh):

time: 195 us -> 195 us (level)
  no operation moved by 1% of the time
where the time goes in v1:
time: 195 us; the launch traced here: 192 us
  starting transfers between devices  49.8 us (26%)
  waiting for transfers between devices  47.8 us (25%)
  matrix products  45.5 us (23%)
  local copies, waits for them, and re-layouts  32.2 us (17%)
  blocking collectives  8.64 us (4%)
  other arithmetic  6.92 us (4%)
    ppermute x12, waiting for transfers between devices, with_halo(): after = lax.ppermute(initial, axis, down)  42.3 us
    dot_general x36, matrix products, convolve(): jnp.einsum('oid,dixyz->oxyz', taps, slab, preferred_element_type=jnp.floa...  38.4 us
    ppermute x12, starting transfers between devices, with_halo(): before = lax.ppermute(last, axis, up)  33.7 us
    ppermute x12, starting transfers between devices, with_halo(): after = lax.ppermute(initial, axis, down)  16.1 us
    slice x4, local copies, waits for them, and re-layouts, convolve(): slab = shifted[:, :, step_x:step_x + depth, step_y:step_y + height, :]  15 us
    dot_general x4, matrix products, convolve(): jnp.einsum('cxyw,wdz->dcxyz', padded, band_table(width), preferred_elemen...  7.04 us
    concatenate x7, other arithmetic, with_halo(): value = jnp.concatenate([before, value, after], axis=dim)  6.71 us
    ppermute x12, waiting for transfers between devices, with_halo(): before = lax.ppermute(last, axis, up)  5.5 us
  transfers between devices with their start and end apart: 24, of which 17 were waited for; matrix products, arithmetic and copies ran while one was open for 3% of the time, Pallas kernels for 0%

profile of v1, /device:TPU:0, one launch (start us, length us, event | category | flops | bytes accessed | tf_op | source)
XLA Modules:
  0.0 191.6 jit_solution(2719549731387878683)
XLA Ops:
  0.0 1.2 copy-done
  1.3 4.9 %collective-permute-start = (bf16[16,1,32,128]{3,2,1,0:T(8,128)(2,1)S(1)}, bf16[16,1,32,128]{3,2,1,0:T(8,128)(2,1)S(1)}, u32[]{:S(2)}, u32[]{:S(2)}) collective-permute-start(bf16[16,1,32,128]{3,2,1,0:T(8,128)(2,1)S(1)} %get-tuple-element.63), channel_id=1, source_target_pairs={{0,8},{1,9},{2,10},{3,11},{4,12},{5,13},{6,14},{7,15},{16,24},{17,... | collective-permute-start | bytes 393224 | tf_op jit(solution)/shard_map/ppermute | solution.py:23
  6.2 1.3 collective-permute-start.1
  7.5 2.1 %all_gather.6 = bf16[2,2,16,16,3,3,3]{3,2,6,5,4,1,0:T(8,128)(2,1)S(1)} all-gather(bf16[1,2,16,16,3,3,3]{3,2,6,5,4,1,0:T(8,128)(2,1)S(1)} %copy-done.2), channel_id=1, replica_groups=mesh['segment'=2,'gx'=2,'gy'=4,'gz'=2] {'segment'}, dimensions={0}, use_global_device_ids=true | all-gather | bytes 82944 | tf_op jit(solution)/shard_map/all_gather | solution.py:64
  9.6 3.4 %collective-permute-done.1 = bf16[16,1,32,128]{3,2,1,0:T(8,128)(2,1)S(1)} collective-permute-done((bf16[16,1,32,128]{3,2,1,0:T(8,128)(2,1)S(1)}, bf16[16,1,32,128]{3,2,1,0:T(8,128)(2,1)S(1)}, u32[]{:S(2)}, u32[]{:S(2)}) %collective-permute-start.1) | collective-permute-done | bytes 131104 | tf_op jit(solution)/shard_map/ppermute | solution.py:24
  13.1 3.5 %collective-permute-start.2 = (bf16[16,6,1,128]{3,2,1,0:T(2,128)(2,1)S(1)}, bf16[16,6,1,128]{3,2,1,0:T(2,128)(2,1)S(1)}, u32[]{:S(2)}, u32[]{:S(2)}) collective-permute-start(bf16[16,6,1,128]{3,2,1,0:T(2,128)(2,1)S(1)} %get-tuple-element.55), channel_id=1, source_target_pairs={{0,2},{2,4},{4,6},{1,3},{3,5},{5,7},{8,10},{10,12},{12,14},{9,11},... | collective-permute-start | bytes 73736 | tf_op jit(solution)/shard_map/ppermute | solution.py:23
  16.6 1.3 collective-permute-start.3
  18.0 1.8 all_gather.7
  19.8 2.8 %collective-permute-done.3 = bf16[16,6,1,128]{3,2,1,0:T(2,128)(2,1)S(1)} collective-permute-done((bf16[16,6,1,128]{3,2,1,0:T(2,128)(2,1)S(1)}, bf16[16,6,1,128]{3,2,1,0:T(2,128)(2,1)S(1)}, u32[]{:S(2)}, u32[]{:S(2)}) %collective-permute-start.3) | collective-permute-done | bytes 24608 | tf_op jit(solution)/shard_map/ppermute | solution.py:24
  24.9 1.3 collective-permute-start.5
  26.2 4.5 %collective-permute-start.4 = (bf16[16,6,34,1]{2,0,3,1:T(8,128)(2,1)S(1)}, bf16[16,6,34,1]{2,0,3,1:T(8,128)(2,1)S(1)}, u32[]{:S(2)}, u32[]{:S(2)}) collective-permute-start(bf16[16,6,34,1]{2,0,3,1:T(8,128)(2,1)S(1)} %copy.44), channel_id=1, source_target_pairs={{0,1},{2,3},{4,5},{6,7},{8,9},{10,11},{12,13},{14,15},{16,17},{18,... | collective-permute-start | bytes 19592 | tf_op jit(solution)/shard_map/ppermute | solution.py:23
  30.8 1.5 collective-permute-done.4
  33.8 2.9 %convert_bitcast_fusion.3 = bf16[3,16,6,34,128]{4,3,2,1,0:T(8,128)(2,1)S(1)} fusion(bf16[16,6,34,1]{3,2,1,0:T(8,128)(2,1)S(1)} %copy.47, bf16[16,6,1,128]{3,2,1,0:T(2,128)(2,1)S(1)} %collective-permute-done.3, bf16[16,1,32,128]{3,2,1,0:T(8,128)(2,1)S(1)} %collective-permute-done.1, bf16[16,4,32,128]{3,2,1,0:T(8,128)(2,1)S(1)} %dynamic-slice_bitcast_fusion, ...), kind=kOutput, calls=%fused_computation.7 | convolution fusion | flops 333271296 | bytes 3355392 | tf_op jit(solution)/shard_map/cxyw,wdz->dcxyz/dot_general | solution.py:41
  36.7 3.7 %fusion.370 = (bf16[3,16,4,32,128]{4,3,2,1,0:T(8,128)(2,1)S(1)}, bf16[3,16,4,32,128]{4,3,2,1,0:T(8,128)(2,1)S(1)}, bf16[3,16,4,32,128]{4,3,2,1,0:T(8,128)(2,1)S(...) fusion(bf16[3,16,6,34,128]{4,3,2,1,0:T(8,128)(2,1)S(1)} %conver, ...), kind=kLoop, calls=%fused_computation.272 | loop fusion | bytes 28311552 | tf_op jit(solution)/shard_map/slice | solution.py:47
  41.4 1.1 fusion.323
  42.5 1.1 fusion.320
  43.6 1.1 fusion.317
  45.7 1.1 fusion.311
  47.9 1.1 fusion.305
  48.9 1.1 fusion.326
  50.1 1.5 collective-permute-start.6
  51.6 1.3 collective-permute-start.7
  52.9 1.2 collective-permute-done.6
  54.1 4.4 %collective-permute-done.7 = bf16[16,1,32,128]{3,0,2,1:T(8,128)(2,1)S(1)} collective-permute-done((bf16[16,1,32,128]{3,0,2,1:T(8,128)(2,1)S(1)}, bf16[16,1,32,128]{3,0,2,1:T(8,128)(2,1)S(1)}, u32[]{:S(2)}, u32[]{:S(2)}) %collective-permute-start.7) | collective-permute-done | bytes 131104 | tf_op jit(solution)/shard_map/ppermute | solution.py:24
  58.4 3.5 %collective-permute-start.8 = (bf16[16,6,1,128]{3,0,2,1:T(8,128)(2,1)S(1)}, bf16[16,6,1,128]{3,0,2,1:T(8,128)(2,1)S(1)}, u32[]{:S(2)}, u32[]{:S(2)}) collective-permute-start(bf16[16,6,1,128]{3,0,2,1:T(8,128)(2,1)S(1)} %get-tuple-element.53), channel_id=1, source_target_pairs={{0,2},{2,4},{4,6},{1,3},{3,5},{5,7},{8,10},{10,12},{12,14},{9,11},... | collective-permute-start | bytes 73736 | tf_op jit(solution)/shard_map/ppermute | solution.py:23
  61.9 1.5 collective-permute-start.9
  63.5 4.2 %collective-permute-done.9 = bf16[16,6,1,128]{3,0,2,1:T(8,128)(2,1)S(1)} collective-permute-done((bf16[16,6,1,128]{3,0,2,1:T(8,128)(2,1)S(1)}, bf16[16,6,1,128]{3,0,2,1:T(8,128)(2,1)S(1)}, u32[]{:S(2)}, u32[]{:S(2)}) %collective-permute-start.9) | collective-permute-done | bytes 24608 | tf_op jit(solution)/shard_map/ppermute | solution.py:24
  69.1 4.2 %collective-permute-start.10 = (bf16[16,6,34,1]{2,0,3,1:T(8,128)(2,1)S(1)}, bf16[16,6,34,1]{2,0,3,1:T(8,128)(2,1)S(1)}, u32[]{:S(2)}, u32[]{:S(2)}) collective-permute-start(bf16[16,6,34,1]{2,0,3,1:T(8,128)(2,1)S(1)} %copy.57), channel_id=1, source_target_pairs={{0,1},{2,3},{4,5},{6,7},{8,9},{10,11},{12,13},{14,15},{16,17},{18,... | collective-permute-start | bytes 19592 | tf_op jit(solution)/shard_map/ppermute | solution.py:23
  74.2 1.3 collective-permute-start.11
  76.3 3.6 %collective-permute-done.11 = bf16[16,6,34,1]{2,0,3,1:T(8,128)(2,1)S(1)} collective-permute-done((bf16[16,6,34,1]{2,0,3,1:T(8,128)(2,1)S(1)}, bf16[16,6,34,1]{2,0,3,1:T(8,128)(2,1)S(1)}, u32[]{:S(2)}, u32[]{:S(2)}) %collective-permute-start.11) | collective-permute-done | bytes 6560 | tf_op jit(solution)/shard_map/ppermute | solution.py:24
  80.7 1.9 pad_maximum_fusion
  82.6 1.4 convert_bitcast_fusion.2
  84.0 4.1 %fusion.369 = (bf16[3,16,4,32,128]{4,3,2,1,0:T(8,128)(2,1)S(1)}, bf16[3,16,4,32,128]{4,3,2,1,0:T(8,128)(2,1)S(1)}, bf16[3,16,4,32,128]{4,3,2,1,0:T(8,128)(2,1)S(...) fusion(bf16[3,16,6,34,128]{4,3,2,1,0:T(8,128)(2,1)S(1)} %conver, ...), kind=kLoop, calls=%fused_computation.271 | loop fusion | bytes 28311552 | tf_op jit(solution)/shard_map/slice | solution.py:47
  96.6 1.1 fusion.329
  97.7 1.5 collective-permute-start.12
  99.2 1.3 collective-permute-start.13
  100.5 1.2 collective-permute-done.12
  101.7 4.4 %collective-permute-done.13 = bf16[16,1,32,128]{3,0,2,1:T(8,128)(2,1)S(1)} collective-permute-done((bf16[16,1,32,128]{3,0,2,1:T(8,128)(2,1)S(1)}, bf16[16,1,32,128]{3,0,2,1:T(8,128)(2,1)S(1)}, u32[]{:S(2)}, u32[]{:S(2)}) %collective-permute-start.13) | collective-permute-done | bytes 131104 | tf_op jit(solution)/shard_map/ppermute | solution.py:24
  106.1 3.5 %collective-permute-start.14 = (bf16[16,6,1,128]{3,0,2,1:T(8,128)(2,1)S(1)}, bf16[16,6,1,128]{3,0,2,1:T(8,128)(2,1)S(1)}, u32[]{:S(2)}, u32[]{:S(2)}) collective-permute-start(bf16[16,6,1,128]{3,0,2,1:T(8,128)(2,1)S(1)} %get-tuple-element.51), channel_id=1, source_target_pairs={{0,2},{2,4},{4,6},{1,3},{3,5},{5,7},{8,10},{10,12},{12,14},{9,11},... | collective-permute-start | bytes 73736 | tf_op jit(solution)/shard_map/ppermute | solution.py:23
  109.6 1.3 collective-permute-start.15
  111.1 4.2 %collective-permute-done.15 = bf16[16,6,1,128]{3,0,2,1:T(8,128)(2,1)S(1)} collective-permute-done((bf16[16,6,1,128]{3,0,2,1:T(8,128)(2,1)S(1)}, bf16[16,6,1,128]{3,0,2,1:T(8,128)(2,1)S(1)}, u32[]{:S(2)}, u32[]{:S(2)}) %collective-permute-start.15) | collective-permute-done | bytes 24608 | tf_op jit(solution)/shard_map/ppermute | solution.py:24
  116.7 1.6 collective-permute-start.16
  119.2 1.5 collective-permute-start.17
  121.5 3.4 %collective-permute-done.17 = bf16[16,6,34,1]{2,0,3,1:T(8,128)(2,1)S(1)} collective-permute-done((bf16[16,6,34,1]{2,0,3,1:T(8,128)(2,1)S(1)}, bf16[16,6,34,1]{2,0,3,1:T(8,128)(2,1)S(1)}, u32[]{:S(2)}, u32[]{:S(2)}) %collective-permute-start.17) | collective-permute-done | bytes 6560 | tf_op jit(solution)/shard_map/ppermute | solution.py:24
  125.8 1.9 pad_maximum_fusion.1
  127.7 1.4 convert_bitcast_fusion.1
  129.0 3.7 %fusion.368 = (bf16[3,16,4,32,128]{4,3,2,1,0:T(8,128)(2,1)S(1)}, bf16[3,16,4,32,128]{4,3,2,1,0:T(8,128)(2,1)S(1)}, bf16[3,16,4,32,128]{4,3,2,1,0:T(8,128)(2,1)S(...) fusion(bf16[3,16,6,34,128]{4,3,2,1,0:T(8,128)(2,1)S(1)} %conver, ...), kind=kLoop, calls=%fused_computation.270 | loop fusion | bytes 28311552 | tf_op jit(solution)/shard_map/slice | solution.py:47
  141.2 1.1 fusion.332
  142.3 1.5 collective-permute-start.18
  143.8 1.3 collective-permute-start.19
  145.1 1.2 collective-permute-done.18
  146.3 4.4 %collective-permute-done.19 = bf16[16,1,32,128]{3,0,2,1:T(8,128)(2,1)S(1)} collective-permute-done((bf16[16,1,32,128]{3,0,2,1:T(8,128)(2,1)S(1)}, bf16[16,1,32,128]{3,0,2,1:T(8,128)(2,1)S(1)}, u32[]{:S(2)}, u32[]{:S(2)}) %collective-permute-start.19) | collective-permute-done | bytes 131104 | tf_op jit(solution)/shard_map/ppermute | solution.py:24
  150.7 1.9 %collective-permute-start.20 = (bf16[16,6,1,128]{3,0,2,1:T(8,128)(2,1)S(1)}, bf16[16,6,1,128]{3,0,2,1:T(8,128)(2,1)S(1)}, u32[]{:S(2)}, u32[]{:S(2)}) collective-permute-start(bf16[16,6,1,128]{3,0,2,1:T(8,128)(2,1)S(1)} %get-tuple-element.49), channel_id=1, source_target_pairs={{0,2},{2,4},{4,6},{1,3},{3,5},{5,7},{8,10},{10,12},{12,14},{9,11},... | collective-permute-start | bytes 73736 | tf_op jit(solution)/shard_map/ppermute | solution.py:23
  152.6 1.3 collective-permute-start.21
  154.1 4.2 %collective-permute-done.21 = bf16[16,6,1,128]{3,0,2,1:T(8,128)(2,1)S(1)} collective-permute-done((bf16[16,6,1,128]{3,0,2,1:T(8,128)(2,1)S(1)}, bf16[16,6,1,128]{3,0,2,1:T(8,128)(2,1)S(1)}, u32[]{:S(2)}, u32[]{:S(2)}) %collective-permute-start.21) | collective-permute-done | bytes 24608 | tf_op jit(solution)/shard_map/ppermute | solution.py:24
  159.8 1.6 collective-permute-start.22
  162.2 1.5 collective-permute-start.23
  164.6 3.4 %collective-permute-done.23 = bf16[16,6,34,1]{2,0,3,1:T(8,128)(2,1)S(1)} collective-permute-done((bf16[16,6,34,1]{2,0,3,1:T(8,128)(2,1)S(1)}, bf16[16,6,34,1]{2,0,3,1:T(8,128)(2,1)S(1)}, u32[]{:S(2)}, u32[]{:S(2)}) %collective-permute-start.23) | collective-permute-done | bytes 6560 | tf_op jit(solution)/shard_map/ppermute | solution.py:24
  168.8 1.9 pad_maximum_fusion.2
  170.7 1.4 convert_bitcast_fusion
  172.1 3.7 %fusion.367 = (bf16[3,16,4,32,128]{4,3,2,1,0:T(8,128)(2,1)S(1)}, bf16[3,16,4,32,128]{4,3,2,1,0:T(8,128)(2,1)S(1)}, bf16[3,16,4,32,128]{4,3,2,1,0:T(8,128)(2,1)S(...) fusion(bf16[3,16,6,34,128]{4,3,2,1,0:T(8,128)(2,1)S(1)} %conver, ...), kind=kLoop, calls=%fused_computation.269 | loop fusion | bytes 28311552 | tf_op jit(solution)/shard_map/slice | solution.py:47
  184.2 1.1 fusion.338
  185.4 4.7 %all_to_all.5 = bf16[2,1,1,16,4,32,128]{6,3,5,4,2,1,0:T(8,128)(2,1)S(1)} all-to-all(bf16[2,1,1,16,4,32,128]{6,3,5,4,2,1,0:T(8,128)(2,1)S(1)} %pad_maximum_fusion.3), channel_id=1, replica_groups=mesh['segment'=2,'gx'=2,'gy'=4,'gz'=2] {'segment'}, dimensions={0} | all-to-all | bytes 2097152 | tf_op jit(solution)/shard_map/all_to_all | solution.py:11
  190.1 1.2 copy.99
  (79 shorter events, 45.0 us)
Async XLA Ops:
  0.0 1.2 copy-start
  0.0 7.5 %copy-start.2 = (bf16[1,2,16,16,3,3,3]{3,2,6,5,4,1,0:T(8,128)(2,1)S(1)}, bf16[1,2,16,16,3,3,3]{3,2,6,5,4,1,0:T(8,128)(2,1)}, u32[]{:S(2)}) copy-start(bf16[1,2,16,16,3,3,3]{3,2,6,5,4,1,0:T(8,128)(2,1)} %param.4) | copy-start | bytes 82948
  1.3 16.7 %copy-start.3 = (bf16[1,2,16]{2,1,0:T(2,128)(2,1)S(1)}, bf16[1,2,16]{2,1,0:T(2,128)(2,1)}, u32[]{:S(2)}) copy-start(bf16[1,2,16]{2,1,0:T(2,128)(2,1)} %param.5) | copy-start | bytes 196
  1.3 8.3 %collective-permute-start = (bf16[16,1,32,128]{3,2,1,0:T(8,128)(2,1)S(1)}, bf16[16,1,32,128]{3,2,1,0:T(8,128)(2,1)S(1)}, u32[]{:S(2)}, u32[]{:S(2)}) collective-permute-start(bf16[16,1,32,128]{3,2,1,0:T(8,128)(2,1)S(1)} %get-tuple-element.63), channel_id=1, source_target_pairs={{0,8},{1,9},{2,10},{3,11},{4,12},{5,13},{6,14},{7,15},{16,24},{17,... | collective-permute-start | bytes 393224 | tf_op jit(solution)/shard_map/ppermute | solution.py:23
  6.2 6.9 %collective-permute-start.1 = (bf16[16,1,32,128]{3,2,1,0:T(8,128)(2,1)S(1)}, bf16[16,1,32,128]{3,2,1,0:T(8,128)(2,1)S(1)}, u32[]{:S(2)}, u32[]{:S(2)}) collective-permute-start(bf16[16,1,32,128]{3,2,1,0:T(8,128)(2,1)S(1)} %get-tuple-element.64), channel_id=1, source_target_pairs={{8,0},{9,1},{10,2},{11,3},{12,4},{13,5},{14,6},{15,7},{24,16},{25,... | collective-permute-start | bytes 393224 | tf_op jit(solution)/shard_map/ppermute | solution.py:24
  13.1 6.7 %collective-permute-start.2 = (bf16[16,6,1,128]{3,2,1,0:T(2,128)(2,1)S(1)}, bf16[16,6,1,128]{3,2,1,0:T(2,128)(2,1)S(1)}, u32[]{:S(2)}, u32[]{:S(2)}) collective-permute-start(bf16[16,6,1,128]{3,2,1,0:T(2,128)(2,1)S(1)} %get-tuple-element.55), channel_id=1, source_target_pairs={{0,2},{2,4},{4,6},{1,3},{3,5},{5,7},{8,10},{10,12},{12,14},{9,11},... | collective-permute-start | bytes 73736 | tf_op jit(solution)/shard_map/ppermute | solution.py:23
  16.6 6.0 %collective-permute-start.3 = (bf16[16,6,1,128]{3,2,1,0:T(2,128)(2,1)S(1)}, bf16[16,6,1,128]{3,2,1,0:T(2,128)(2,1)S(1)}, u32[]{:S(2)}, u32[]{:S(2)}) collective-permute-start(bf16[16,6,1,128]{3,2,1,0:T(2,128)(2,1)S(1)} %get-tuple-element.56), channel_id=1, source_target_pairs={{2,0},{4,2},{6,4},{3,1},{5,3},{7,5},{10,8},{12,10},{14,12},{11,9},... | collective-permute-start | bytes 73736 | tf_op jit(solution)/shard_map/ppermute | solution.py:24
  24.9 8.1 %collective-permute-start.5 = (bf16[16,6,34,1]{2,0,3,1:T(8,128)(2,1)S(1)}, bf16[16,6,34,1]{2,0,3,1:T(8,128)(2,1)S(1)}, u32[]{:S(2)}, u32[]{:S(2)}) collective-permute-start(bf16[16,6,34,1]{2,0,3,1:T(8,128)(2,1)S(1)} %copy.45), channel_id=1, source_target_pairs={{1,0},{3,2},{5,4},{7,6},{9,8},{11,10},{13,12},{15,14},{17,16},{19,... | collective-permute-start | bytes 19592 | tf_op jit(solution)/shard_map/ppermute | solution.py:24
  26.2 6.1 %collective-permute-start.4 = (bf16[16,6,34,1]{2,0,3,1:T(8,128)(2,1)S(1)}, bf16[16,6,34,1]{2,0,3,1:T(8,128)(2,1)S(1)}, u32[]{:S(2)}, u32[]{:S(2)}) collective-permute-start(bf16[16,6,34,1]{2,0,3,1:T(8,128)(2,1)S(1)} %copy.44), channel_id=1, source_target_pairs={{0,1},{2,3},{4,5},{6,7},{8,9},{10,11},{12,13},{14,15},{16,17},{18,... | collective-permute-start | bytes 19592 | tf_op jit(solution)/shard_map/ppermute | solution.py:23
  50.1 4.0 %collective-permute-start.6 = (bf16[16,1,32,128]{3,0,2,1:T(8,128)(2,1)S(1)}, bf16[16,1,32,128]{3,0,2,1:T(8,128)(2,1)S(1)}, u32[]{:S(2)}, u32[]{:S(2)}) collective-permute-start(bf16[16,1,32,128]{3,0,2,1:T(8,128)(2,1)S(1)} %get-tuple-element.61), channel_id=1, source_target_pairs={{0,8},{1,9},{2,10},{3,11},{4,12},{5,13},{6,14},{7,15},{16,24},{17,... | collective-permute-start | bytes 393224 | tf_op jit(solution)/shard_map/ppermute | solution.py:23
  51.6 6.9 %collective-permute-start.7 = (bf16[16,1,32,128]{3,0,2,1:T(8,128)(2,1)S(1)}, bf16[16,1,32,128]{3,0,2,1:T(8,128)(2,1)S(1)}, u32[]{:S(2)}, u32[]{:S(2)}) collective-permute-start(bf16[16,1,32,128]{3,0,2,1:T(8,128)(2,1)S(1)} %get-tuple-element.62), channel_id=1, source_target_pairs={{8,0},{9,1},{10,2},{11,3},{12,4},{13,5},{14,6},{15,7},{24,16},{25,... | collective-permute-start | bytes 393224 | tf_op jit(solution)/shard_map/ppermute | solution.py:24
  58.4 5.0 %collective-permute-start.8 = (bf16[16,6,1,128]{3,0,2,1:T(8,128)(2,1)S(1)}, bf16[16,6,1,128]{3,0,2,1:T(8,128)(2,1)S(1)}, u32[]{:S(2)}, u32[]{:S(2)}) collective-permute-start(bf16[16,6,1,128]{3,0,2,1:T(8,128)(2,1)S(1)} %get-tuple-element.53), channel_id=1, source_target_pairs={{0,2},{2,4},{4,6},{1,3},{3,5},{5,7},{8,10},{10,12},{12,14},{9,11},... | collective-permute-start | bytes 73736 | tf_op jit(solution)/shard_map/ppermute | solution.py:23
  61.9 5.7 %collective-permute-start.9 = (bf16[16,6,1,128]{3,0,2,1:T(8,128)(2,1)S(1)}, bf16[16,6,1,128]{3,0,2,1:T(8,128)(2,1)S(1)}, u32[]{:S(2)}, u32[]{:S(2)}) collective-permute-start(bf16[16,6,1,128]{3,0,2,1:T(8,128)(2,1)S(1)} %get-tuple-element.54), channel_id=1, source_target_pairs={{2,0},{4,2},{6,4},{3,1},{5,3},{7,5},{10,8},{12,10},{14,12},{11,9},... | collective-permute-start | bytes 73736 | tf_op jit(solution)/shard_map/ppermute | solution.py:24
  69.1 6.4 %collective-permute-start.10 = (bf16[16,6,34,1]{2,0,3,1:T(8,128)(2,1)S(1)}, bf16[16,6,34,1]{2,0,3,1:T(8,128)(2,1)S(1)}, u32[]{:S(2)}, u32[]{:S(2)}) collective-permute-start(bf16[16,6,34,1]{2,0,3,1:T(8,128)(2,1)S(1)} %copy.57), channel_id=1, source_target_pairs={{0,1},{2,3},{4,5},{6,7},{8,9},{10,11},{12,13},{14,15},{16,17},{18,... | collective-permute-start | bytes 19592 | tf_op jit(solution)/shard_map/ppermute | solution.py:23
  74.2 5.7 %collective-permute-start.11 = (bf16[16,6,34,1]{2,0,3,1:T(8,128)(2,1)S(1)}, bf16[16,6,34,1]{2,0,3,1:T(8,128)(2,1)S(1)}, u32[]{:S(2)}, u32[]{:S(2)}) collective-permute-start(bf16[16,6,34,1]{2,0,3,1:T(8,128)(2,1)S(1)} %copy.58), channel_id=1, source_target_pairs={{1,0},{3,2},{5,4},{7,6},{9,8},{11,10},{13,12},{15,14},{17,16},{19,... | collective-permute-start | bytes 19592 | tf_op jit(solution)/shard_map/ppermute | solution.py:24
  97.7 4.0 %collective-permute-start.12 = (bf16[16,1,32,128]{3,0,2,1:T(8,128)(2,1)S(1)}, bf16[16,1,32,128]{3,0,2,1:T(8,128)(2,1)S(1)}, u32[]{:S(2)}, u32[]{:S(2)}) collective-permute-start(bf16[16,1,32,128]{3,0,2,1:T(8,128)(2,1)S(1)} %get-tuple-element.59), channel_id=1, source_target_pairs={{0,8},{1,9},{2,10},{3,11},{4,12},{5,13},{6,14},{7,15},{16,24},{17,... | collective-permute-start | bytes 393224 | tf_op jit(solution)/shard_map/ppermute | solution.py:23
  99.2 6.9 %collective-permute-start.13 = (bf16[16,1,32,128]{3,0,2,1:T(8,128)(2,1)S(1)}, bf16[16,1,32,128]{3,0,2,1:T(8,128)(2,1)S(1)}, u32[]{:S(2)}, u32[]{:S(2)}) collective-permute-start(bf16[16,1,32,128]{3,0,2,1:T(8,128)(2,1)S(1)} %get-tuple-element.60), channel_id=1, source_target_pairs={{8,0},{9,1},{10,2},{11,3},{12,4},{13,5},{14,6},{15,7},{24,16},{25,... | collective-permute-start | bytes 393224 | tf_op jit(solution)/shard_map/ppermute | solution.py:24
  106.1 5.0 %collective-permute-start.14 = (bf16[16,6,1,128]{3,0,2,1:T(8,128)(2,1)S(1)}, bf16[16,6,1,128]{3,0,2,1:T(8,128)(2,1)S(1)}, u32[]{:S(2)}, u32[]{:S(2)}) collective-permute-start(bf16[16,6,1,128]{3,0,2,1:T(8,128)(2,1)S(1)} %get-tuple-element.51), channel_id=1, source_target_pairs={{0,2},{2,4},{4,6},{1,3},{3,5},{5,7},{8,10},{10,12},{12,14},{9,11},... | collective-permute-start | bytes 73736 | tf_op jit(solution)/shard_map/ppermute | solution.py:23
  109.6 5.7 %collective-permute-start.15 = (bf16[16,6,1,128]{3,0,2,1:T(8,128)(2,1)S(1)}, bf16[16,6,1,128]{3,0,2,1:T(8,128)(2,1)S(1)}, u32[]{:S(2)}, u32[]{:S(2)}) collective-permute-start(bf16[16,6,1,128]{3,0,2,1:T(8,128)(2,1)S(1)} %get-tuple-element.52), channel_id=1, source_target_pairs={{2,0},{4,2},{6,4},{3,1},{5,3},{7,5},{10,8},{12,10},{14,12},{11,9},... | collective-permute-start | bytes 73736 | tf_op jit(solution)/shard_map/ppermute | solution.py:24
  116.7 4.0 %collective-permute-start.16 = (bf16[16,6,34,1]{2,0,3,1:T(8,128)(2,1)S(1)}, bf16[16,6,34,1]{2,0,3,1:T(8,128)(2,1)S(1)}, u32[]{:S(2)}, u32[]{:S(2)}) collective-permute-start(bf16[16,6,34,1]{2,0,3,1:T(8,128)(2,1)S(1)} %copy.71), channel_id=1, source_target_pairs={{0,1},{2,3},{4,5},{6,7},{8,9},{10,11},{12,13},{14,15},{16,17},{18,... | collective-permute-start | bytes 19592 | tf_op jit(solution)/shard_map/ppermute | solution.py:23
  119.2 5.7 %collective-permute-start.17 = (bf16[16,6,34,1]{2,0,3,1:T(8,128)(2,1)S(1)}, bf16[16,6,34,1]{2,0,3,1:T(8,128)(2,1)S(1)}, u32[]{:S(2)}, u32[]{:S(2)}) collective-permute-start(bf16[16,6,34,1]{2,0,3,1:T(8,128)(2,1)S(1)} %copy.72), channel_id=1, source_target_pairs={{1,0},{3,2},{5,4},{7,6},{9,8},{11,10},{13,12},{15,14},{17,16},{19,... | collective-permute-start | bytes 19592 | tf_op jit(solution)/shard_map/ppermute | solution.py:24
  142.3 4.0 %collective-permute-start.18 = (bf16[16,1,32,128]{3,0,2,1:T(8,128)(2,1)S(1)}, bf16[16,1,32,128]{3,0,2,1:T(8,128)(2,1)S(1)}, u32[]{:S(2)}, u32[]{:S(2)}) collective-permute-start(bf16[16,1,32,128]{3,0,2,1:T(8,128)(2,1)S(1)} %get-tuple-element.57), channel_id=1, source_target_pairs={{0,8},{1,9},{2,10},{3,11},{4,12},{5,13},{6,14},{7,15},{16,24},{17,... | collective-permute-start | bytes 393224 | tf_op jit(solution)/shard_map/ppermute | solution.py:23
  143.8 6.9 %collective-permute-start.19 = (bf16[16,1,32,128]{3,0,2,1:T(8,128)(2,1)S(1)}, bf16[16,1,32,128]{3,0,2,1:T(8,128)(2,1)S(1)}, u32[]{:S(2)}, u32[]{:S(2)}) collective-permute-start(bf16[16,1,32,128]{3,0,2,1:T(8,128)(2,1)S(1)} %get-tuple-element.58), channel_id=1, source_target_pairs={{8,0},{9,1},{10,2},{11,3},{12,4},{13,5},{14,6},{15,7},{24,16},{25,... | collective-permute-start | bytes 393224 | tf_op jit(solution)/shard_map/ppermute | solution.py:24
  150.7 3.4 %collective-permute-start.20 = (bf16[16,6,1,128]{3,0,2,1:T(8,128)(2,1)S(1)}, bf16[16,6,1,128]{3,0,2,1:T(8,128)(2,1)S(1)}, u32[]{:S(2)}, u32[]{:S(2)}) collective-permute-start(bf16[16,6,1,128]{3,0,2,1:T(8,128)(2,1)S(1)} %get-tuple-element.49), channel_id=1, source_target_pairs={{0,2},{2,4},{4,6},{1,3},{3,5},{5,7},{8,10},{10,12},{12,14},{9,11},... | collective-permute-start | bytes 73736 | tf_op jit(solution)/shard_map/ppermute | solution.py:23
  152.6 5.7 %collective-permute-start.21 = (bf16[16,6,1,128]{3,0,2,1:T(8,128)(2,1)S(1)}, bf16[16,6,1,128]{3,0,2,1:T(8,128)(2,1)S(1)}, u32[]{:S(2)}, u32[]{:S(2)}) collective-permute-start(bf16[16,6,1,128]{3,0,2,1:T(8,128)(2,1)S(1)} %get-tuple-element.50), channel_id=1, source_target_pairs={{2,0},{4,2},{6,4},{3,1},{5,3},{7,5},{10,8},{12,10},{14,12},{11,9},... | collective-permute-start | bytes 73736 | tf_op jit(solution)/shard_map/ppermute | solution.py:24
  159.8 4.0 %collective-permute-start.22 = (bf16[16,6,34,1]{2,0,3,1:T(8,128)(2,1)S(1)}, bf16[16,6,34,1]{2,0,3,1:T(8,128)(2,1)S(1)}, u32[]{:S(2)}, u32[]{:S(2)}) collective-permute-start(bf16[16,6,34,1]{2,0,3,1:T(8,128)(2,1)S(1)} %copy.85), channel_id=1, source_target_pairs={{0,1},{2,3},{4,5},{6,7},{8,9},{10,11},{12,13},{14,15},{16,17},{18,... | collective-permute-start | bytes 19592 | tf_op jit(solution)/shard_map/ppermute | solution.py:23
  162.2 5.7 %collective-permute-start.23 = (bf16[16,6,34,1]{2,0,3,1:T(8,128)(2,1)S(1)}, bf16[16,6,34,1]{2,0,3,1:T(8,128)(2,1)S(1)}, u32[]{:S(2)}, u32[]{:S(2)}) collective-permute-start(bf16[16,6,34,1]{2,0,3,1:T(8,128)(2,1)S(1)} %copy.86), channel_id=1, source_target_pairs={{1,0},{3,2},{5,4},{7,6},{9,8},{11,10},{13,12},{15,14},{17,16},{19,... | collective-permute-start | bytes 19592 | tf_op jit(solution)/shard_map/ppermute | solution.py:24
  185.4 6.0 %copy-start.1 = (bf16[2,16,4,32,128]{4,3,2,1,0:T(8,128)(2,1)S(1)}, bf16[2,16,4,32,128]{4,3,2,1,0:T(8,128)(2,1)}, u32[]{:S(2)}) copy-start(bf16[2,16,4,32,128]{4,3,2,1,0:T(8,128)(2,1)} %param.3) | copy-start | bytes 3145732
